TPU v7x, 32 devices: a whole 2x2x4 slice. The times are simulated.
32 devices in a mesh: dp: 8 (over z, x), tensor: 4 (over y, core).
Axes of the slice: x: 2, y: 2, z: 4, core: 2. Of those that a mesh axis runs over, the one named last changes fastest.
Arguments:
- tokens: bfloat16 [16384, 768], P(('dp', 'tensor')), may hold values from -6 to 6
- stack: bfloat16 [4, 16384, 768], P(None, ('dp', 'tensor')), may hold values from -6 to 6
- cotangent: bfloat16 [16384, 768], P(('dp', 'tensor')), may hold values from -6 to 6
- starts: int32 [16, 2], P('dp'), may hold values from 0 to 768
- w_query: bfloat16 [768, 768], P('dp', 'tensor'), may hold values from -0.21875 to 0.21875
- w_key: bfloat16 [768, 768], P('dp', 'tensor'), may hold values from -0.21875 to 0.21875
- w_value: bfloat16 [768, 768], P('dp', 'tensor'), may hold values from -0.21875 to 0.21875
- w_output: bfloat16 [768, 768], P('tensor', 'dp'), may hold values from -0.875 to 0.875
- w_in: bfloat16 [768, 3072], P('dp', 'tensor'), may hold values from -0.21875 to 0.21875
- w_out: bfloat16 [3072, 768], P('tensor', 'dp'), may hold values from -0.109375 to 0.109375
- gain_one: float32 [768], replicated, may hold values from 0.1 to 1.9
- shift_one: float32 [768], replicated, may hold values from -3 to 3
- gain_two: float32 [768], replicated, may hold values from 0.1 to 1.9
- shift_two: float32 [768], replicated, may hold values from -3 to 3
- bias_in: float32 [3072], replicated, may hold values from -3 to 3
- bias_out: float32 [768], replicated, may hold values from -3 to 3
- depth_weights: float32 [5], replicated, may hold values from 0.3 to 1.2
Outputs:
- layer_out: bfloat16 [16384, 768], P(('dp', 'tensor'))
- grad_tokens: float32 [16384, 768], P(('dp', 'tensor'))
- grad_stack: float32 [4, 16384, 768], P(None, ('dp', 'tensor'))
- grad_w_query: float32 [768, 768], P('dp', 'tensor')
- grad_w_key: float32 [768, 768], P('dp', 'tensor')
- grad_w_value: float32 [768, 768], P('dp', 'tensor')
- grad_w_output: float32 [768, 768], P('tensor', 'dp')
- grad_w_in: float32 [768, 3072], P('dp', 'tensor')
- grad_w_out: float32 [3072, 768], P('tensor', 'dp')
- grad_gain_one: float32 [768], replicated
- grad_shift_one: float32 [768], replicated
- grad_gain_two: float32 [768], replicated
- grad_shift_two: float32 [768], replicated
- grad_bias_in: float32 [3072], replicated
- grad_bias_out: float32 [768], replicated
- grad_depth: float32 [5], replicated
All inputs are finite; a program needn't handle non-finite values.
Results may differ from a plain program's by a relative error of at most 0.012.
Values may be sent and summed in bfloat16 or wider, within the bound.
A program may use at most 128 MiB of HBM per device.

v0:
```python
import math
import jax
import jax.numpy as jnp
from jax import lax
from jax.sharding import PartitionSpec as P

HEAD_DIM = 64
PIECE = 256
EPSILON = 1e-05
NEGATIVE = -1e30


def layer_norm(values, gain, shift):
    centre = values - jnp.mean(values, axis=-1, keepdims=True)
    spread = jnp.mean(centre * centre, axis=-1, keepdims=True)
    return centre * lax.rsqrt(spread + EPSILON) * gain + shift


def tables(seq_length, head_size):
    half_dim = head_size // 2
    frequency = jnp.exp(
        -jnp.log(10000.0) * jnp.arange(half_dim, dtype=jnp.float32) * 2.0 / head_size
    )
    angles = jnp.arange(seq_length, dtype=jnp.float32)[:, None] * frequency[None, :]
    return (jnp.cos(angles), jnp.sin(angles))


def rotate(values, cosine_table, sine_table):
    half_dim = values.shape[-1] // 2
    front_half = values[..., :half_dim]
    back_half = values[..., half_dim:]
    cosines = cosine_table[:, None, :]
    sine_rows = sine_table[:, None, :]
    return jnp.concatenate(
        [
            front_half * cosines - back_half * sine_rows,
            back_half * cosines + front_half * sine_rows,
        ],
        axis=-1,
    )


def allowed_mask(starts, seq_length, piece_size):
    position = jnp.arange(seq_length, dtype=jnp.int32)
    inside = (position[None, None, :] >= starts[:, :, None]) & (
        position[None, None, :] < starts[:, :, None] + piece_size
    )
    jointly = jnp.any(inside[:, :, :, None] & inside[:, :, None, :], axis=1)
    return jointly | (position[None, :, None] >= position[None, None, :])


def gelu_tanh(values):
    return jax.nn.gelu(values, approximate=True)


def right_transposed(matrix, weight):
    return lax.dot_general(
        matrix, weight, (((1,), (1,)), ((), ())), preferred_element_type=jnp.float32
    )


def left_transposed(matrix, other):
    return lax.dot_general(
        matrix, other, (((0,), (0,)), ((), ())), preferred_element_type=jnp.float32
    )


def attend_forward(query, key_rows, value_rows, allowed, score_scale):

    def one_sequence(entries):
        query_seq, key_seq, value_seq, allowed_seq = entries
        scores = (
            jnp.einsum("qhd,khd->hqk", query_seq, key_seq, preferred_element_type=jnp.float32)
            * score_scale
        )
        scores = jnp.where(allowed_seq[None], scores, NEGATIVE)
        highest = jnp.max(scores, axis=-1, keepdims=True)
        powers = jnp.exp(scores - highest)
        row_total = jnp.sum(powers, axis=-1, keepdims=True)
        attention = (powers / row_total).astype(jnp.bfloat16)
        mixed_rows = jnp.einsum(
            "hqk,khd->qhd", attention, value_seq, preferred_element_type=jnp.float32
        )
        return (mixed_rows.astype(jnp.bfloat16), highest + jnp.log(row_total))

    return lax.map(one_sequence, (query, key_rows, value_rows, allowed))


def attend_backward(query, key_rows, value_rows, grad_mixed, log_totals, allowed, score_scale):

    def one_sequence(entries):
        query_seq, key_seq, value_seq, grad_seq, log_seq, allowed_seq = entries
        scores = (
            jnp.einsum("qhd,khd->hqk", query_seq, key_seq, preferred_element_type=jnp.float32)
            * score_scale
        )
        scores = jnp.where(allowed_seq[None], scores, NEGATIVE)
        attention = jnp.exp(scores - log_seq)
        grad_value = jnp.einsum(
            "hqk,qhd->khd",
            attention.astype(jnp.bfloat16),
            grad_seq,
            preferred_element_type=jnp.float32,
        )
        grad_attention = jnp.einsum(
            "qhd,khd->hqk", grad_seq, value_seq, preferred_element_type=jnp.float32
        )
        row_delta = jnp.sum(attention * grad_attention, axis=-1, keepdims=True)
        grad_scores = (attention * (grad_attention - row_delta)).astype(jnp.bfloat16)
        grad_query = (
            jnp.einsum("hqk,khd->qhd", grad_scores, key_seq, preferred_element_type=jnp.float32)
            * score_scale
        )
        grad_key = (
            jnp.einsum("hqk,qhd->khd", grad_scores, query_seq, preferred_element_type=jnp.float32)
            * score_scale
        )
        return (grad_query, grad_key, grad_value.astype(jnp.bfloat16))

    return lax.map(one_sequence, (query, key_rows, value_rows, grad_mixed, log_totals, allowed))


def per_device(
    tokens,
    stack,
    cotangent,
    starts,
    w_query,
    w_key,
    w_value,
    w_output,
    w_in,
    w_out,
    gain_one,
    shift_one,
    gain_two,
    shift_two,
    bias_in,
    bias_out,
    depth_weights,
):
    rows_here = tokens.shape[0]
    features = tokens.shape[1]
    groups = lax.axis_size("tensor")
    position = lax.axis_index("tensor")
    seq_count = starts.shape[0]
    seq_length = rows_here * groups // seq_count
    score_scale = 1.0 / math.sqrt(HEAD_DIM)
    local_heads = w_query.shape[1] // HEAD_DIM
    hidden = w_in.shape[1]
    cosine_table, sine_table = tables(seq_length, HEAD_DIM)
    allowed = allowed_mask(starts, seq_length, PIECE)

    def to_heads(matrix):
        return matrix.reshape(seq_count, seq_length, local_heads, HEAD_DIM)

    def from_heads(blocks):
        return blocks.reshape(seq_count * seq_length, local_heads * HEAD_DIM)

    def share_rows(local_rows):
        return lax.all_gather(local_rows, "tensor", axis=0, tiled=True)

    def share_grad(local_rows):
        return lax.all_gather(local_rows, "tensor", axis=0, tiled=True)

    def merge_rows(source, weight):
        return lax.psum_scatter(
            jnp.dot(source, weight, preferred_element_type=jnp.float32),
            "tensor",
            scatter_dimension=0,
            tiled=True,
        )

    def return_rows(pairs):
        running = jnp.zeros((lax.axis_size("tensor") * rows_here, features), jnp.float32)
        for source, weight in pairs:
            running = running + right_transposed(source, weight)
        return lax.psum_scatter(running, "tensor", scatter_dimension=0, tiled=True)

    query_w, key_w, value_w, output_w = (
        lax.all_gather(w_query, "dp", axis=0, tiled=True),
        lax.all_gather(w_key, "dp", axis=0, tiled=True),
        lax.all_gather(w_value, "dp", axis=0, tiled=True),
        lax.all_gather(w_output, "dp", axis=1, tiled=True),
    )
    inner_w, outer_w = (
        lax.all_gather(w_in, "dp", axis=0, tiled=True),
        lax.all_gather(w_out, "dp", axis=1, tiled=True),
    )
    token_rows = tokens.astype(jnp.float32)
    normed_one = layer_norm(token_rows, gain_one, shift_one).astype(jnp.bfloat16)
    normed_all = share_rows(normed_one)
    query = rotate(
        to_heads(jnp.dot(normed_all, query_w, preferred_element_type=jnp.float32)),
        cosine_table,
        sine_table,
    ).astype(jnp.bfloat16)
    key_rows = rotate(
        to_heads(jnp.dot(normed_all, key_w, preferred_element_type=jnp.float32)),
        cosine_table,
        sine_table,
    ).astype(jnp.bfloat16)
    value_rows = to_heads(jnp.dot(normed_all, value_w, preferred_element_type=jnp.float32)).astype(
        jnp.bfloat16
    )
    mixed_heads, log_totals = attend_forward(query, key_rows, value_rows, allowed, score_scale)
    mixed_flat = from_heads(mixed_heads)
    middle = token_rows + merge_rows(mixed_flat, output_w)
    normed_two = layer_norm(middle, gain_two, shift_two).astype(jnp.bfloat16)
    second_all = share_rows(normed_two)
    bias_slice = lax.dynamic_slice_in_dim(bias_in, position * hidden, hidden)
    pre_act = jnp.dot(second_all, inner_w, preferred_element_type=jnp.float32) + bias_slice
    activated = gelu_tanh(pre_act).astype(jnp.bfloat16)
    block_out = middle + merge_rows(activated, outer_w) + bias_out
    averaged = depth_weights[4] * block_out
    for layer_index in range(4):
        averaged = averaged + depth_weights[layer_index] * stack[layer_index].astype(jnp.float32)
    layer_out = averaged.astype(jnp.bfloat16)
    grad_rows = cotangent.astype(jnp.float32)
    grad_stack = jnp.stack([depth_weights[layer_index] * grad_rows for layer_index in range(4)])
    depth_terms = jnp.stack(
        [jnp.sum(stack[layer_index].astype(jnp.float32) * grad_rows) for layer_index in range(4)]
        + [jnp.sum(block_out * grad_rows)]
    )
    grad_block = depth_weights[4] * grad_rows
    grad_bias_out = jnp.sum(grad_block, axis=0)
    grad_sent = share_grad(grad_block.astype(jnp.bfloat16))
    grad_outer = left_transposed(activated, grad_sent)
    grad_act = right_transposed(grad_sent, outer_w)
    grad_pre = jax.vjp(gelu_tanh, pre_act)[1](grad_act)[0].astype(jnp.bfloat16)
    grad_bias_slice = jnp.sum(grad_pre.astype(jnp.float32), axis=0)
    bias_full = lax.dynamic_update_slice_in_dim(
        jnp.zeros((bias_in.shape[0],), jnp.float32), grad_bias_slice, position * hidden, 0
    )
    grad_inner = left_transposed(second_all, grad_pre)
    grad_norm_two = return_rows(((grad_pre, inner_w),))
    layer_two = jax.vjp(layer_norm, middle, gain_two, shift_two)[1](grad_norm_two)
    grad_middle = grad_block + layer_two[0]
    grad_attn_sent = share_grad(grad_middle.astype(jnp.bfloat16))
    grad_output_w = left_transposed(mixed_flat, grad_attn_sent)
    grad_mixed = right_transposed(grad_attn_sent, output_w).astype(jnp.bfloat16)
    grad_query, grad_key, grad_value = attend_backward(
        query, key_rows, value_rows, to_heads(grad_mixed), log_totals, allowed, score_scale
    )
    grad_query = from_heads(rotate(grad_query, cosine_table, -sine_table)).astype(jnp.bfloat16)
    grad_key = from_heads(rotate(grad_key, cosine_table, -sine_table)).astype(jnp.bfloat16)
    grad_value = from_heads(grad_value)
    grad_query_w = left_transposed(normed_all, grad_query)
    grad_key_w = left_transposed(normed_all, grad_key)
    grad_value_w = left_transposed(normed_all, grad_value)
    grad_norm_one = return_rows(((grad_query, query_w), (grad_key, key_w), (grad_value, value_w)))
    layer_one = jax.vjp(layer_norm, token_rows, gain_one, shift_one)[1](grad_norm_one)
    grad_tokens = grad_middle + layer_one[0]
    grad_w_query, grad_w_key, grad_w_value, grad_w_output, grad_w_in, grad_w_out = (
        lax.psum_scatter(grad_query_w, "dp", scatter_dimension=0, tiled=True),
        lax.psum_scatter(grad_key_w, "dp", scatter_dimension=0, tiled=True),
        lax.psum_scatter(grad_value_w, "dp", scatter_dimension=0, tiled=True),
        lax.psum_scatter(grad_output_w, "dp", scatter_dimension=1, tiled=True),
        lax.psum_scatter(grad_inner, "dp", scatter_dimension=0, tiled=True),
        lax.psum_scatter(grad_outer, "dp", scatter_dimension=1, tiled=True),
    )
    summed = lax.psum(
        (
            layer_one[1],
            layer_one[2],
            layer_two[1],
            layer_two[2],
            bias_full,
            grad_bias_out,
            depth_terms,
        ),
        ("dp", "tensor"),
    )
    return (
        layer_out,
        grad_tokens,
        grad_stack,
        grad_w_query,
        grad_w_key,
        grad_w_value,
        grad_w_output,
        grad_w_in,
        grad_w_out,
        summed[0],
        summed[1],
        summed[2],
        summed[3],
        summed[4],
        summed[5],
        summed[6],
    )


def solution(mesh):
    in_specs = (
        P(("dp", "tensor"), None),
        P(None, ("dp", "tensor"), None),
        P(("dp", "tensor"), None),
        P("dp", None),
        P("dp", "tensor"),
        P("dp", "tensor"),
        P("dp", "tensor"),
        P("tensor", "dp"),
        P("dp", "tensor"),
        P("tensor", "dp"),
        P(),
        P(),
        P(),
        P(),
        P(),
        P(),
        P(),
    )
    out_specs = (
        P(("dp", "tensor"), None),
        P(("dp", "tensor"), None),
        P(None, ("dp", "tensor"), None),
        P("dp", "tensor"),
        P("dp", "tensor"),
        P("dp", "tensor"),
        P("tensor", "dp"),
        P("dp", "tensor"),
        P("tensor", "dp"),
        P(),
        P(),
        P(),
        P(),
        P(),
        P(),
        P(),
    )
    return jax.shard_map(
        per_device, mesh=mesh, in_specs=in_specs, out_specs=out_specs, check_vma=False
    )
```

profile of v0, /device:TPU:0, one launch (start us, length us, event | category | flops | bytes accessed | tf_op | source)
XLA Modules:
  0.0 1099.3 jit_solution(18201807398381428645)
XLA Ops:
  14.7 2.9 and_reduce_fusion
  18.9 4.5 copy.84
  23.3 34.9 %all_gather.34 = bf16[192,768]{0,1:T(8,128)(2,1)} all-gather(bf16[192,96]{0,1:T(8,128)(2,1)S(1)} %copy.86), channel_id=1, replica_groups=mesh['dp'=8,'tensor'=4] {'dp'}, dimensions={1}, use_global_device_ids=true | all-gather | bytes 331776 | tf_op jit(solution)/shard_map/all_gather | solution.py:184
  58.3 33.1 %all_gather.32 = bf16[768,192]{1,0:T(8,128)(2,1)} all-gather(bf16[96,192]{1,0:T(8,128)(2,1)S(1)} %copy-done.46), channel_id=1, replica_groups=mesh['dp'=8,'tensor'=4] {'dp'}, dimensions={0}, use_global_device_ids=true | all-gather | bytes 331776 | tf_op jit(solution)/shard_map/all_gather | solution.py:181
  91.4 31.1 %all_gather.33 = bf16[768,192]{1,0:T(8,128)(2,1)S(1)} all-gather(bf16[96,192]{1,0:T(8,128)(2,1)S(1)} %copy-done.47), channel_id=1, replica_groups=mesh['dp'=8,'tensor'=4] {'dp'}, dimensions={0}, use_global_device_ids=true | all-gather | bytes 331776 | tf_op jit(solution)/shard_map/all_gather | solution.py:182
  122.5 33.5 %all_gather.31 = bf16[768,192]{1,0:T(8,128)(2,1)} all-gather(bf16[96,192]{1,0:T(8,128)(2,1)S(1)} %copy-done.48), channel_id=1, replica_groups=mesh['dp'=8,'tensor'=4] {'dp'}, dimensions={0}, use_global_device_ids=true | all-gather | bytes 331776 | tf_op jit(solution)/shard_map/all_gather | solution.py:183
  157.3 4.2 convolution_convert_fusion.1
  161.5 3.2 convert_element_type.101
  164.7 2.2 copy.83
  166.9 2.3 fusion.107
  169.3 3.4 reshape.244
  172.7 3.2 fusion.103
  175.9 2.3 fusion.106
  178.2 2.6 reshape.243
  185.7 29.1 %while.26 = (s32[]{:T(128)}, bf16[2,1024,3,64]{1,3,2,0:T(8,128)(2,1)}, f32[2,3,1024,1]{2,1,3,0:T(4,128)}, bf16[2,1024,3,64]{1,3,2,0:T(8,128)(2,1)}, pred[2,1024,...) while((s32[]{:T(128)}, ...), condition=%wide.region_6.7_spmd, body=%wide.region_3.6_spmd.sunk | while | flops 843248640 | bytes 55154872 | solution.py:86
  187.5 2.6 fusion.174
  190.1 3.9 fusion.175
  194.0 5.7 fusion.176
  202.0 2.6 fusion.174
  204.6 3.9 fusion.175
  208.5 5.7 fusion.176
  214.8 2.0 copy.85
  217.9 3.8 fusion.108
  222.3 59.0 %reduce-scatter.13.cloned.1.call-done = f32[512,768]{1,0:T(8,128)} async-done(((f32[2048,768]{1,0:T(8,128)}), f32[512,768]{1,0:T(8,128)}) %reduce-scatter.13.cloned.1.call-update) | async-done | bytes 1572880 | tf_op jit(solution)/shard_map/reduce_scatter | solution.py:167
  288.3 24.7 %all-gather.9.cloned.1.call-done = bf16[2048,768]{1,0:T(8,128)(2,1)} async-done(((bf16[512,768]{1,0:T(8,128)(2,1)}), bf16[2048,768]{1,0:T(8,128)(2,1)}) %all-gather.9.cloned.1.call-update) | async-done | bytes 3145744 | tf_op jit(solution)/shard_map/all_gather | solution.py:161
  313.0 7.5 fusion.109
  320.6 36.3 %all-gather.13.cloned.1.call-done = bf16[768,768]{0,1:T(8,128)(2,1)} async-done(((bf16[768,96]{0,1:T(8,128)(2,1)}), bf16[768,768]{0,1:T(8,128)(2,1)}) %all-gather.13.cloned.1.call-update) | async-done | bytes 1179664 | tf_op jit(solution)/shard_map/all_gather | solution.py:188
  356.9 29.1 %all-gather.15.cloned.1.call-done = bf16[2048,768]{1,0:T(8,128)(2,1)} async-done(((bf16[512,768]{1,0:T(8,128)(2,1)}), bf16[2048,768]{1,0:T(8,128)(2,1)}) %all-gather.15.cloned.1.call-update) | async-done | bytes 3145744 | tf_op jit(solution)/shard_map/all_gather | solution.py:164
  386.0 11.1 %convert_reduce_fusion = (f32[768]{0:T(1024)}, bf16[2048,768]{1,0:T(8,128)(2,1)S(1)}, bf16[2048,768]{1,0:T(8,128)(2,1)}) fusion(f32[2048,768]{1,0:T(8,128)} %fusion.109, f32[768]{0:T(1024)S(1)} %dynamic_slice.36, bf16[2048,768]{1,0:T(8,128)(2,1)} %all-gather.15.cloned.1.call-done, bf16[768,768]{0,1:T(8,128)(2,1)} %all-gather.13.cloned.1.call-done), kind=kOutput, calls=%fused_computation.73 | convolution fusion | flops 2455239936 | bytes 16914432 | tf_op jit(solution)/shard_map/dot_general | solution.py:57
  398.8 4.5 fusion.111
  403.4 8.0 fusion.110
  411.5 50.2 %reduce-scatter.17.cloned.1.call-done = f32[512,768]{1,0:T(8,128)} async-done(((f32[2048,768]{1,0:T(8,128)}), f32[512,768]{1,0:T(8,128)}) %reduce-scatter.17.cloned.1.call-update) | async-done | bytes 1572880 | tf_op jit(solution)/shard_map/reduce_scatter | solution.py:178
  461.7 60.8 %reduce-scatter.15.cloned.1.call-done = f32[512,768]{1,0:T(8,128)} async-done(((f32[2048,768]{1,0:T(8,128)}), f32[512,768]{1,0:T(8,128)}) %reduce-scatter.15.cloned.1.call-update) | async-done | bytes 1572880 | tf_op jit(solution)/shard_map/reduce_scatter | solution.py:167
  522.5 8.1 multiply_reduce_fusion.1
  534.4 28.6 %all-gather.17.cloned.1.call-done = bf16[2048,768]{1,0:T(8,128)(2,1)} async-done(((bf16[512,768]{1,0:T(8,128)(2,1)}), bf16[2048,768]{1,0:T(8,128)(2,1)}) %all-gather.17.cloned.1.call-update) | async-done | bytes 3145744 | tf_op jit(solution)/shard_map/all_gather | solution.py:164
  563.0 3.1 convolution_convert_fusion
  569.9 51.6 %while.27 = (s32[]{:T(128)}, f32[2,1024,3,64]{1,3,2,0:T(8,128)}, f32[2,1024,3,64]{1,3,2,0:T(8,128)}, bf16[2,1024,3,64]{1,3,2,0:T(8,128)(2,1)}, bf16[2,1024,3,64]...) while((s32[]{:T(128)}, f32[2,1024,3,64]{1,3,2,0:T(8,128)}, ...), condition=%wide.region_16.17_spmd, body=%wide.region_14.16_spmd.sunk | while | flops 2061038592 | bytes 135890256 | solution.py:120
  573.5 3.7 fusion.188
  577.2 7.1 multiply_reduce_fusion.5
  584.4 7.1 multiply_convert_fusion.3
  591.5 2.0 fusion.187
  599.1 3.7 fusion.188
  602.8 7.1 multiply_reduce_fusion.5
  610.0 7.1 multiply_convert_fusion.3
  617.1 2.0 fusion.187
  621.5 4.5 convolution_bitcast_fusion
  633.5 3.8 add_add_fusion
  639.3 6.0 fusion.117
  645.6 7.1 fusion.118
  652.7 3.0 fusion.116
  655.9 3.1 fusion.115
  659.4 4.1 fusion.114
  663.5 25.3 %reduce-scatter.31.cloned.1.call-done = f32[96,192]{1,0:T(8,128)} async-done(((f32[768,192]{1,0:T(8,128)}), f32[96,192]{1,0:T(8,128)}) %reduce-scatter.31.cloned.1.call-update) | async-done | bytes 73744
  690.4 58.6 %reduce-scatter.19.cloned.1.call-done = f32[512,768]{1,0:T(8,128)} async-done(((f32[2048,768]{1,0:T(8,128)}), f32[512,768]{1,0:T(8,128)}) %reduce-scatter.19.cloned.1.call-update) | async-done | bytes 1572880 | tf_op jit(solution)/shard_map/reduce_scatter | solution.py:178
  749.0 2.0 fusion.99
  751.9 8.8 fusion.90
  760.7 3.4 stack.43
  764.1 40.7 %all-reduce = (f32[768]{0:T(1024)}, f32[768]{0:T(1024)}, f32[768]{0:T(1024)}, f32[768]{0:T(1024)}, f32[3072]{0:T(1024)}, /*index=5*/f32[768]{0:T(1024)}, f32[5]{0:T(128)}) all-reduce(f32[768]{0:T(1024)S(1)} %get-tuple-element.187, f32[768]{0:T(1024)S(1)} %get-tuple-element.191, ...), channel_id=1, replica_groups=mesh['dp'=8,'tensor'=4] {'dp','tensor'}, use_global_device_ids=true, to_apply=%region_27.28 | all-reduce | flops 6917 | bytes 55336 | tf_op jit(solution)/shard_map/psum | solution.py:262
  804.8 4.6 pad_maximum_fusion
  809.4 13.0 %reduce-scatter.27.cloned.1.call-done = f32[96,768]{1,0:T(8,128)} async-done(((f32[768,768]{1,0:T(8,128)}), f32[96,768]{1,0:T(8,128)}) %reduce-scatter.27.cloned.1.call-update) | async-done | bytes 294928 | tf_op jit(solution)/shard_map/reduce_scatter | solution.py:259
  822.5 72.5 %reduce-scatter.29.cloned.1.call-done = f32[768,96]{0,1:T(8,128)} async-done(((f32[768,768]{0,1:T(8,128)}), f32[768,96]{0,1:T(8,128)}) %reduce-scatter.29.cloned.1.call-update) | async-done | bytes 294928 | tf_op jit(solution)/shard_map/reduce_scatter | solution.py:260
  894.9 65.7 %reduce-scatter.25.cloned.1.call-done = f32[96,192]{1,0:T(8,128)} async-done(((f32[768,192]{1,0:T(8,128)}), f32[96,192]{1,0:T(8,128)}) %reduce-scatter.25.cloned.1.call-update) | async-done | bytes 73744 | tf_op jit(solution)/shard_map/reduce_scatter | solution.py:257
  960.7 65.4 %reduce-scatter.23.cloned.1.call-done = f32[96,192]{1,0:T(8,128)} async-done(((f32[768,192]{1,0:T(8,128)}), f32[96,192]{1,0:T(8,128)}) %reduce-scatter.23.cloned.1.call-update) | async-done | bytes 73744 | tf_op jit(solution)/shard_map/reduce_scatter | solution.py:256
  1026.1 65.6 %reduce-scatter.21.cloned.1.call-done = f32[96,192]{1,0:T(8,128)} async-done(((f32[768,192]{1,0:T(8,128)}), f32[96,192]{1,0:T(8,128)}) %reduce-scatter.21.cloned.1.call-update) | async-done | bytes 73744 | tf_op jit(solution)/shard_map/reduce_scatter | solution.py:255
  (250 shorter events, 59.9 us)
Async XLA Ops:
  8.0 4.1 copy-start.1
  8.0 6.2 copy-start.49
  8.0 149.3 %all-gather.7.cloned.1.call-start = ((), (), s32[]{:S(2)}) async-start(), calls=%async_computation.10 | async-start | bytes 3932160 | tf_op jit(solution)/shard_map/all_gather | solution.py:161
  9.5 2.1 copy-start.43
  9.5 5.1 copy-start.62
  14.1 267.2 %reduce-scatter.13.cloned.1.call-start = ((), (), s32[]{:S(2)}) async-start(), calls=%async_computation.11 | async-start | bytes 7864320 | tf_op jit(solution)/shard_map/reduce_scatter | solution.py:167
  18.8 39.5 %copy-start.46 = (bf16[96,192]{1,0:T(8,128)(2,1)S(1)}, bf16[96,192]{1,0:T(8,128)(2,1)}, u32[]{:S(2)}) copy-start(bf16[96,192]{1,0:T(8,128)(2,1)} %param.25) | copy-start | bytes 110596
  18.8 72.5 %copy-start.47 = (bf16[96,192]{1,0:T(8,128)(2,1)S(1)}, bf16[96,192]{1,0:T(8,128)(2,1)}, u32[]{:S(2)}) copy-start(bf16[96,192]{1,0:T(8,128)(2,1)} %param.26) | copy-start | bytes 110596
  18.8 103.6 %copy-start.48 = (bf16[96,192]{1,0:T(8,128)(2,1)S(1)}, bf16[96,192]{1,0:T(8,128)(2,1)}, u32[]{:S(2)}) copy-start(bf16[96,192]{1,0:T(8,128)(2,1)} %param.27) | copy-start | bytes 110596
  122.5 44.4 %copy-start.20 = (bf16[768,192]{1,0:T(8,128)(2,1)}, bf16[768,192]{1,0:T(8,128)(2,1)S(1)}, u32[]{:S(2)}) copy-start(bf16[768,192]{1,0:T(8,128)(2,1)S(1)} %all_gather.33) | copy-start | bytes 884740
  157.3 9.6 copy-start.8
  172.7 3.2 copy-start.22
  187.5 2.6 copy-start
  202.0 2.6 copy-start
  214.8 3.1 copy-start.24
  221.7 59.7 %copy-start.2 = (bf16[512,768]{1,0:T(8,128)(2,1)S(1)}, bf16[512,768]{1,0:T(8,128)(2,1)}, u32[]{:S(2)}) copy-start(bf16[512,768]{1,0:T(8,128)(2,1)} %param.21) | copy-start | bytes 2359300
  221.7 66.6 %all-gather.11.cloned.1.call-start = ((), (), s32[]{:S(2)}) async-start(), calls=%async_computation.13 | async-start | bytes 1327104 | tf_op jit(solution)/shard_map/all_gather | solution.py:187
  222.3 61.0 %copy-start.50 = (f32[768]{0:T(1024)S(1)}, f32[768]{0:T(1024)}, u32[]{:S(2)}) copy-start(f32[768]{0:T(1024)} %param.33) | copy-start | bytes 9220
  222.3 61.0 %copy-start.60 = (f32[768]{0:T(1024)S(1)}, f32[768]{0:T(1024)}, u32[]{:S(2)}) copy-start(f32[768]{0:T(1024)} %param.34) | copy-start | bytes 9220
  222.3 90.8 %all-gather.9.cloned.1.call-start = ((), (), s32[]{:S(2)}) async-start(), calls=%async_computation.12 | async-start | bytes 3932160 | tf_op jit(solution)/shard_map/all_gather | solution.py:161
  283.0 2.2 copy-start.59
  283.0 2.8 copy-start.13
  284.5 72.4 %all-gather.13.cloned.1.call-start = ((), (), s32[]{:S(2)}) async-start(), calls=%async_computation.14 | async-start | bytes 1327104 | tf_op jit(solution)/shard_map/all_gather | solution.py:188
  285.1 100.9 %all-gather.15.cloned.1.call-start = ((), (), s32[]{:S(2)}) async-start(), calls=%async_computation.16 | async-start | bytes 3932160 | tf_op jit(solution)/shard_map/all_gather | solution.py:164
  287.5 174.2 %reduce-scatter.17.cloned.1.call-start = ((), (), s32[]{:S(2)}) async-start(), calls=%async_computation.17 | async-start | bytes 7864320 | tf_op jit(solution)/shard_map/reduce_scatter | solution.py:178
  386.0 12.8 %copy-start.65 = (bf16[768,768]{1,0:T(8,128)(2,1)S(1)}, bf16[768,768]{1,0:T(8,128)(2,1)}, u32[]{:S(2)}) copy-start(bf16[768,768]{1,0:T(8,128)(2,1)} %all-gather.11.cloned.1.call-done) | copy-start | bytes 3538948
  403.3 119.2 %reduce-scatter.15.cloned.1.call-start = ((), (), s32[]{:S(2)}) async-start(), calls=%async_computation.15 | async-start | bytes 7864320 | tf_op jit(solution)/shard_map/reduce_scatter | solution.py:167
  411.4 111.1 %copy-start.61 = (f32[768]{0:T(1024)S(1)}, f32[768]{0:T(1024)}, u32[]{:S(2)}) copy-start(f32[768]{0:T(1024)} %param.36) | copy-start | bytes 9220
  411.4 151.5 %all-gather.17.cloned.1.call-start = ((), (), s32[]{:S(2)}) async-start(), calls=%async_computation.18 | async-start | bytes 3932160 | tf_op jit(solution)/shard_map/all_gather | solution.py:164
  522.5 8.1 copy-start.16
  534.3 154.5 %reduce-scatter.31.cloned.1.call-start = ((), (), s32[]{:S(2)}) async-start(), calls=%async_computation.25 | async-start | bytes 884736
  566.1 3.8 copy-start.5
  566.1 3.8 copy-start.7
  566.1 3.8 copy-start.15
  567.6 2.3 copy-start.42
  577.2 7.1 copy-start.30
  584.4 7.1 copy-start.32
  591.5 2.1 copy-start.35
  602.8 7.1 copy-start.30
  610.0 7.1 copy-start.32
  621.5 4.8 copy-start.34
  621.5 4.8 copy-start.37
  621.5 4.8 copy-start.39
  621.5 4.8 copy-start.40
  626.0 122.9 %reduce-scatter.19.cloned.1.call-start = ((), (), s32[]{:S(2)}) async-start(), calls=%async_computation.19 | async-start | bytes 7864320 | tf_op jit(solution)/shard_map/reduce_scatter | solution.py:178
  631.2 2.1 copy-start.26
  637.4 185.1 %reduce-scatter.27.cloned.1.call-start = ((), (), s32[]{:S(2)}) async-start(), calls=%async_computation.23 | async-start | bytes 2654208 | tf_op jit(solution)/shard_map/reduce_scatter | solution.py:259
  645.3 249.7 %reduce-scatter.29.cloned.1.call-start = ((), (), s32[]{:S(2)}) async-start(), calls=%async_computation.24 | async-start | bytes 2654208 | tf_op jit(solution)/shard_map/reduce_scatter | solution.py:260
  645.6 7.2 copy-start.9
  652.7 308.0 %reduce-scatter.25.cloned.1.call-start = ((), (), s32[]{:S(2)}) async-start(), calls=%async_computation.22 | async-start | bytes 884736 | tf_op jit(solution)/shard_map/reduce_scatter | solution.py:257
  655.8 3.2 copy-start.63
  655.8 370.3 %reduce-scatter.23.cloned.1.call-start = ((), (), s32[]{:S(2)}) async-start(), calls=%async_computation.21 | async-start | bytes 884736 | tf_op jit(solution)/shard_map/reduce_scatter | solution.py:256
  659.0 432.8 %reduce-scatter.21.cloned.1.call-start = ((), (), s32[]{:S(2)}) async-start(), calls=%async_computation.20 | async-start | bytes 884736 | tf_op jit(solution)/shard_map/reduce_scatter | solution.py:255
  659.3 89.6 %copy-start.3 = (bf16[512,768]{1,0:T(8,128)(2,1)S(1)}, bf16[512,768]{1,0:T(8,128)(2,1)}, u32[]{:S(2)}) copy-start(bf16[512,768]{1,0:T(8,128)(2,1)} %param.21) | copy-start | bytes 2359300
  659.3 89.6 %copy-start.44 = (f32[512]{0:T(512)S(1)}, f32[512]{0:T(512)}, u32[]{:S(2)}) copy-start(f32[512]{0:T(512)} %copy-done.43) | copy-start | bytes 6148
  659.3 89.6 %copy-start.45 = (f32[768]{0:T(1024)S(1)}, f32[768]{0:T(1024)}, u32[]{:S(2)}) copy-start(f32[768]{0:T(1024)} %param.31) | copy-start | bytes 9220
  663.4 87.6 %copy-start.56 = (f32[512]{0:T(512)S(1)}, f32[512]{0:T(512)}, u32[]{:S(2)}) copy-start(f32[512]{0:T(512)} %copy-done.55) | copy-start | bytes 6148
  663.4 87.6 %copy-start.52 = (f32[512]{0:T(512)S(1)}, f32[512]{0:T(512)}, u32[]{:S(2)}) copy-start(f32[512]{0:T(512)} %copy-done.51) | copy-start | bytes 6148
  690.4 61.5 %copy-start.14 = (bf16[512,768]{1,0:T(8,128)(2,1)S(1)}, bf16[512,768]{1,0:T(8,128)(2,1)}, u32[]{:S(2)}) copy-start(bf16[512,768]{1,0:T(8,128)(2,1)} %param.23) | copy-start | bytes 2359300
  690.4 61.5 %copy-start.54 = (f32[512]{0:T(512)S(1)}, f32[512]{0:T(512)}, u32[]{:S(2)}) copy-start(f32[512]{0:T(512)} %copy-done.53) | copy-start | bytes 6148
  749.0 2.1 copy-start.10
  749.0 2.9 copy-start.12
  751.9 12.2 %copy-start.57 = (f32[768]{0:T(1024)S(1)}, f32[768]{0:T(1024)}, u32[]{:S(2)}) copy-start(f32[768]{0:T(1024)} %get-tuple-element.185) | copy-start | bytes 9220
  751.9 12.2 %copy-start.58 = (f32[768]{0:T(1024)S(1)}, f32[768]{0:T(1024)}, u32[]{:S(2)}) copy-start(f32[768]{0:T(1024)} %get-tuple-element.190) | copy-start | bytes 9220
  (28 other events, 37.0 us)
Sparse Core Ops, SparseCore 0:
  14.2 31.2 all-gather.6
  221.8 59.4 reduce-scatter.12
  534.4 28.5 all-gather.16
Sparse Core Ops, SparseCore 1:
  224.3 42.6 all-gather.10
  284.6 28.4 all-gather.8
  315.3 41.5 all-gather.12
  359.1 26.8 all-gather.14
  403.4 58.2 reduce-scatter.16
  464.2 58.2 reduce-scatter.14
  626.1 62.6 reduce-scatter.30
  691.7 57.2 reduce-scatter.18
  753.3 69.1 reduce-scatter.26
  826.9 67.9 reduce-scatter.28
  899.0 61.6 reduce-scatter.24
  964.6 61.5 reduce-scatter.22
  1030.2 61.5 reduce-scatter.20
where the time goes:
time: 1110 us; the launch traced here: 1100 us
  waiting for transfers between devices  656 us (59%)
  blocking collectives  173 us (16%)
  matrix products  129 us (12%)
  other arithmetic  68.3 us (6%)
  local copies, waits for them, and re-layouts  53.7 us (5%)
  between operations  16.6 us (1%)
    reduce_scatter x2, waiting for transfers between devices, merge_rows(): lax.psum_scatter(jnp.dot(source, weight, preferred_element_type=jnp.float...  120 us
    reduce_scatter x2, waiting for transfers between devices, return_rows(): return lax.psum_scatter(running, 'tensor', scatter_dimension=0, tiled=True)  109 us
    reduce_scatter x1, waiting for transfers between devices, per_device(): lax.psum_scatter(grad_outer, 'dp', scatter_dimension=1, tiled=True)  72.5 us
    reduce_scatter x1, waiting for transfers between devices, per_device(): lax.psum_scatter(grad_value_w, 'dp', scatter_dimension=0, tiled=True)  65.7 us
    reduce_scatter x1, waiting for transfers between devices, per_device(): lax.psum_scatter(grad_query_w, 'dp', scatter_dimension=0, tiled=True)  65.6 us
    reduce_scatter x1, waiting for transfers between devices, per_device(): lax.psum_scatter(grad_key_w, 'dp', scatter_dimension=0, tiled=True)  65.4 us
    all_gather x2, waiting for transfers between devices, share_grad(): return lax.all_gather(local_rows, 'tensor', axis=0, tiled=True)  57.7 us
    psum x1, blocking collectives, per_device(): lax.psum((layer_one[1], layer_one[2], layer_two[1], layer_two[2], bias_fu...  40.7 us
  transfers between devices with their start and end apart: 16, of which 14 were waited for; matrix products, arithmetic and copies ran while one was open for 8% of the time, Pallas kernels for 0%

commit v1 on v0

--- a/solution.py
+++ b/solution.py
@@ -177,11 +177,39 @@
             running = running + right_transposed(source, weight)
         return lax.psum_scatter(running, "tensor", scatter_dimension=0, tiled=True)
 
+    def tiles_spread(inp, bus_axis):
+        o_now, work_now, mixed_arr = (lax.psum(1, bus_axis), lax.axis_index(bus_axis), inp.shape[1])
+        vec_out = lax.dynamic_update_slice_in_dim(
+            jnp.zeros(
+                tuple((pp * o_now if tick == 1 else pp for tick, pp in enumerate(inp.shape))),
+                inp.dtype,
+            ),
+            inp,
+            work_now * mixed_arr,
+            axis=1,
+        )
+        ready = f_now = inp
+        for dd in range(1, o_now // 2 + 1):
+            ready = lax.ppermute(
+                ready, bus_axis, tuple(((tick, (tick + 1) % o_now) for tick in range(o_now)))
+            )
+            vec_out = lax.dynamic_update_slice_in_dim(
+                vec_out, ready, (work_now - dd) % o_now * mixed_arr, axis=1
+            )
+            if 2 * dd < o_now:
+                f_now = lax.ppermute(
+                    f_now, bus_axis, tuple(((tick, (tick - 1) % o_now) for tick in range(o_now)))
+                )
+                vec_out = lax.dynamic_update_slice_in_dim(
+                    vec_out, f_now, (work_now + dd) % o_now * mixed_arr, axis=1
+                )
+        return vec_out
+
     query_w, key_w, value_w, output_w = (
         lax.all_gather(w_query, "dp", axis=0, tiled=True),
         lax.all_gather(w_key, "dp", axis=0, tiled=True),
         lax.all_gather(w_value, "dp", axis=0, tiled=True),
-        lax.all_gather(w_output, "dp", axis=1, tiled=True),
+        tiles_spread(w_output, "dp"),
     )
     inner_w, outer_w = (
         lax.all_gather(w_in, "dp", axis=0, tiled=True),

time: 1110 us -> 1090 us (0.982)
  blocking collectives: 173 us -> 139 us
  starting transfers between devices: 1.07 us -> 16.4 us
    all_gather x1 -> x0, blocking collectives: 34.9 us -> none  [per_device(): lax.all_gather(w_output, 'dp', axis=1, tiled=True)]
    ppermute x0 -> x7, starting transfers between devices: none -> 14.7 us  [the longest x3 14.7 us: tiles_spread(): lax.ppermute(f_now, bus_axis, tuple(((tick, (tick - 1) % o_now) for tick...]
  transfers between devices with their start and end apart: 16 -> 23, of which waited for: 14 -> 15; matrix products, arithmetic and copies ran while one was open for 8% -> 8% of each run, Pallas kernels for 0% -> 0%
where the time goes in v1:
time: 1090 us; the launch traced here: 1080 us
  waiting for transfers between devices  657 us (60%)
  blocking collectives  139 us (13%)
  matrix products  130 us (12%)
  other arithmetic  67.8 us (6%)
  local copies, waits for them, and re-layouts  56.9 us (5%)
  between operations  16.7 us (2%)
  starting transfers between devices  16.4 us (2%)
    reduce_scatter x2, waiting for transfers between devices, merge_rows(): lax.psum_scatter(jnp.dot(source, weight, preferred_element_type=jnp.float...  120 us
    reduce_scatter x2, waiting for transfers between devices, return_rows(): return lax.psum_scatter(running, 'tensor', scatter_dimension=0, tiled=True)  109 us
    reduce_scatter x1, waiting for transfers between devices, per_device(): lax.psum_scatter(grad_outer, 'dp', scatter_dimension=1, tiled=True)  72.6 us
    reduce_scatter x1, waiting for transfers between devices, per_device(): lax.psum_scatter(grad_value_w, 'dp', scatter_dimension=0, tiled=True)  65.7 us
    reduce_scatter x1, waiting for transfers between devices, per_device(): lax.psum_scatter(grad_query_w, 'dp', scatter_dimension=0, tiled=True)  65.7 us
    reduce_scatter x1, waiting for transfers between devices, per_device(): lax.psum_scatter(grad_key_w, 'dp', scatter_dimension=0, tiled=True)  65.5 us
    all_gather x2, waiting for transfers between devices, share_grad(): return lax.all_gather(local_rows, 'tensor', axis=0, tiled=True)  57.3 us
    psum x1, blocking collectives, per_device(): lax.psum((layer_one[1], layer_one[2], layer_two[1], layer_two[2], bias_fu...  40.8 us
  transfers between devices with their start and end apart: 23, of which 15 were waited for; matrix products, arithmetic and copies ran while one was open for 8% of the time, Pallas kernels for 0%

profile of v1, /device:TPU:0, one launch (start us, length us, event | category | flops | bytes accessed | tf_op | source)
XLA Modules:
  0.0 1084.3 jit_solution(3797597194403206540)
XLA Ops:
  13.1 6.0 collective-permute-start.1
  19.5 2.9 and_reduce_fusion
  25.9 32.2 %all_gather.29 = bf16[768,192]{1,0:T(8,128)(2,1)S(1)} all-gather(bf16[96,192]{1,0:T(8,128)(2,1)S(1)} %copy-done.46), channel_id=1, replica_groups=mesh['dp'=8,'tensor'=4] {'dp'}, dimensions={0}, use_global_device_ids=true | all-gather | bytes 331776 | tf_op jit(solution)/shard_map/all_gather | solution.py:209
  58.1 3.9 collective-permute-start.3
  62.0 33.0 %all_gather.30 = bf16[768,192]{1,0:T(8,128)(2,1)} all-gather(bf16[96,192]{1,0:T(8,128)(2,1)S(1)} %copy-done.47), channel_id=1, replica_groups=mesh['dp'=8,'tensor'=4] {'dp'}, dimensions={0}, use_global_device_ids=true | all-gather | bytes 331776 | tf_op jit(solution)/shard_map/all_gather | solution.py:210
  95.0 4.8 collective-permute-start.5
  99.8 33.4 %all_gather.28 = bf16[768,192]{1,0:T(8,128)(2,1)} all-gather(bf16[96,192]{1,0:T(8,128)(2,1)S(1)} %copy-done.48), channel_id=1, replica_groups=mesh['dp'=8,'tensor'=4] {'dp'}, dimensions={0}, use_global_device_ids=true | all-gather | bytes 331776 | tf_op jit(solution)/shard_map/all_gather | solution.py:211
  133.2 4.4 copy.83
  142.2 4.2 convolution_convert_fusion.1
  146.3 3.2 convert_element_type.101
  149.6 2.2 copy.82
  151.8 3.3 fusion.107
  155.1 3.4 reshape.244
  158.5 3.2 fusion.103
  161.7 2.3 fusion.106
  164.0 2.8 reshape.243
  171.7 27.8 %while.26 = (s32[]{:T(128)}, bf16[2,1024,3,64]{1,3,2,0:T(8,128)(2,1)}, f32[2,3,1024,1]{2,1,3,0:T(4,128)S(1)}, bf16[2,1024,3,64]{1,3,2,0:T(8,128)(2,1)}, pred[2,1...) while((s32[]{:T(128)}, ...), condition=%wide.region_6.7_spmd, body=%wide.region_3.6_spmd.sunk | while | flops 843248640 | bytes 55163064 | solution.py:86
  173.3 2.6 fusion.174
  175.9 3.9 fusion.175
  179.8 5.7 fusion.176
  187.2 2.6 fusion.174
  189.8 3.9 fusion.175
  193.7 5.7 fusion.176
  202.5 3.7 fusion.108
  207.0 59.3 %reduce-scatter.13.cloned.1.call-done = f32[512,768]{1,0:T(8,128)} async-done(((f32[2048,768]{1,0:T(8,128)}), f32[512,768]{1,0:T(8,128)}) %reduce-scatter.13.cloned.1.call-update) | async-done | bytes 1572880 | tf_op jit(solution)/shard_map/reduce_scatter | solution.py:167
  273.6 24.4 %all-gather.9.cloned.1.call-done = bf16[2048,768]{1,0:T(8,128)(2,1)} async-done(((bf16[512,768]{1,0:T(8,128)(2,1)}), bf16[2048,768]{1,0:T(8,128)(2,1)}) %all-gather.9.cloned.1.call-update) | async-done | bytes 3145744 | tf_op jit(solution)/shard_map/all_gather | solution.py:161
  298.0 7.5 fusion.109
  305.5 36.3 %all-gather.13.cloned.1.call-done = bf16[768,768]{0,1:T(8,128)(2,1)} async-done(((bf16[768,96]{0,1:T(8,128)(2,1)}), bf16[768,768]{0,1:T(8,128)(2,1)}) %all-gather.13.cloned.1.call-update) | async-done | bytes 1179664 | tf_op jit(solution)/shard_map/all_gather | solution.py:216
  341.8 29.1 %all-gather.15.cloned.1.call-done = bf16[2048,768]{1,0:T(8,128)(2,1)} async-done(((bf16[512,768]{1,0:T(8,128)(2,1)}), bf16[2048,768]{1,0:T(8,128)(2,1)}) %all-gather.15.cloned.1.call-update) | async-done | bytes 3145744 | tf_op jit(solution)/shard_map/all_gather | solution.py:164
  370.9 10.9 %convert_reduce_fusion = (f32[768]{0:T(1024)}, bf16[2048,768]{1,0:T(8,128)(2,1)S(1)}, bf16[2048,768]{1,0:T(8,128)(2,1)}) fusion(f32[2048,768]{1,0:T(8,128)} %fusion.109, f32[768]{0:T(1024)S(1)} %dynamic_slice.36, bf16[2048,768]{1,0:T(8,128)(2,1)} %all-gather.15.cloned.1.call-done, bf16[768,768]{0,1:T(8,128)(2,1)} %all-gather.13.cloned.1.call-done), kind=kOutput, calls=%fused_computation.73 | convolution fusion | flops 2455239936 | bytes 16914432 | tf_op jit(solution)/shard_map/dot_general | solution.py:57
  383.5 4.5 fusion.111
  388.1 8.0 fusion.110
  396.2 50.2 %reduce-scatter.17.cloned.1.call-done = f32[512,768]{1,0:T(8,128)} async-done(((f32[2048,768]{1,0:T(8,128)}), f32[512,768]{1,0:T(8,128)}) %reduce-scatter.17.cloned.1.call-update) | async-done | bytes 1572880 | tf_op jit(solution)/shard_map/reduce_scatter | solution.py:178
  446.4 60.8 %reduce-scatter.15.cloned.1.call-done = f32[512,768]{1,0:T(8,128)} async-done(((f32[2048,768]{1,0:T(8,128)}), f32[512,768]{1,0:T(8,128)}) %reduce-scatter.15.cloned.1.call-update) | async-done | bytes 1572880 | tf_op jit(solution)/shard_map/reduce_scatter | solution.py:167
  507.2 8.4 multiply_reduce_fusion.1
  519.8 28.2 %all-gather.17.cloned.1.call-done = bf16[2048,768]{1,0:T(8,128)(2,1)} async-done(((bf16[512,768]{1,0:T(8,128)(2,1)}), bf16[2048,768]{1,0:T(8,128)(2,1)}) %all-gather.17.cloned.1.call-update) | async-done | bytes 3145744 | tf_op jit(solution)/shard_map/all_gather | solution.py:164
  548.0 3.1 convolution_convert_fusion
  554.9 51.3 %while.27 = (s32[]{:T(128)}, f32[2,1024,3,64]{1,3,2,0:T(8,128)}, f32[2,1024,3,64]{1,3,2,0:T(8,128)}, bf16[2,1024,3,64]{1,3,2,0:T(8,128)(2,1)}, bf16[2,1024,3,64]...) while((s32[]{:T(128)}, f32[2,1024,3,64]{1,3,2,0:T(8,128)}, ...), condition=%wide.region_16.17_spmd, body=%wide.region_14.16_spmd.sunk | while | flops 2061038592 | bytes 135890256 | solution.py:120
  558.1 3.7 fusion.188
  561.8 7.2 multiply_reduce_fusion.5
  569.0 7.1 multiply_convert_fusion.3
  576.1 2.0 fusion.187
  583.7 3.7 fusion.188
  587.4 7.2 multiply_reduce_fusion.5
  594.6 7.1 multiply_convert_fusion.3
  601.7 2.0 fusion.187
  606.2 4.5 convolution_bitcast_fusion
  618.2 3.8 add_add_fusion
  623.9 6.0 fusion.117
  630.2 7.1 fusion.118
  637.4 3.1 fusion.116
  640.5 3.0 fusion.115
  644.0 4.1 fusion.114
  648.1 25.2 %reduce-scatter.31.cloned.1.call-done = f32[96,192]{1,0:T(8,128)} async-done(((f32[768,192]{1,0:T(8,128)}), f32[96,192]{1,0:T(8,128)}) %reduce-scatter.31.cloned.1.call-update) | async-done | bytes 73744
  674.9 58.7 %reduce-scatter.19.cloned.1.call-done = f32[512,768]{1,0:T(8,128)} async-done(((f32[2048,768]{1,0:T(8,128)}), f32[512,768]{1,0:T(8,128)}) %reduce-scatter.19.cloned.1.call-update) | async-done | bytes 1572880 | tf_op jit(solution)/shard_map/reduce_scatter | solution.py:178
  736.5 9.1 fusion.90
  745.6 3.3 stack.43
  748.9 40.8 %all-reduce = (f32[768]{0:T(1024)}, f32[768]{0:T(1024)}, f32[768]{0:T(1024)}, f32[768]{0:T(1024)}, f32[3072]{0:T(1024)}, /*index=5*/f32[768]{0:T(1024)}, f32[5]{0:T(128)}) all-reduce(f32[768]{0:T(1024)S(1)} %get-tuple-element.187, f32[768]{0:T(1024)S(1)} %get-tuple-element.191, ...), channel_id=1, replica_groups=mesh['dp'=8,'tensor'=4] {'dp','tensor'}, use_global_device_ids=true, to_apply=%region_27.28 | all-reduce | flops 6917 | bytes 55336 | tf_op jit(solution)/shard_map/psum | solution.py:290
  789.7 4.6 pad_maximum_fusion
  794.3 12.9 %reduce-scatter.27.cloned.1.call-done = f32[96,768]{1,0:T(8,128)} async-done(((f32[768,768]{1,0:T(8,128)}), f32[96,768]{1,0:T(8,128)}) %reduce-scatter.27.cloned.1.call-update) | async-done | bytes 294928 | tf_op jit(solution)/shard_map/reduce_scatter | solution.py:287
  807.2 72.6 %reduce-scatter.29.cloned.1.call-done = f32[768,96]{0,1:T(8,128)} async-done(((f32[768,768]{0,1:T(8,128)}), f32[768,96]{0,1:T(8,128)}) %reduce-scatter.29.cloned.1.call-update) | async-done | bytes 294928 | tf_op jit(solution)/shard_map/reduce_scatter | solution.py:288
  879.8 65.7 %reduce-scatter.25.cloned.1.call-done = f32[96,192]{1,0:T(8,128)} async-done(((f32[768,192]{1,0:T(8,128)}), f32[96,192]{1,0:T(8,128)}) %reduce-scatter.25.cloned.1.call-update) | async-done | bytes 73744 | tf_op jit(solution)/shard_map/reduce_scatter | solution.py:285
  945.6 65.5 %reduce-scatter.23.cloned.1.call-done = f32[96,192]{1,0:T(8,128)} async-done(((f32[768,192]{1,0:T(8,128)}), f32[96,192]{1,0:T(8,128)}) %reduce-scatter.23.cloned.1.call-update) | async-done | bytes 73744 | tf_op jit(solution)/shard_map/reduce_scatter | solution.py:284
  1011.1 65.7 %reduce-scatter.21.cloned.1.call-done = f32[96,192]{1,0:T(8,128)} async-done(((f32[768,192]{1,0:T(8,128)}), f32[96,192]{1,0:T(8,128)}) %reduce-scatter.21.cloned.1.call-update) | async-done | bytes 73744 | tf_op jit(solution)/shard_map/reduce_scatter | solution.py:283
  (271 shorter events, 67.5 us)
Async XLA Ops:
  8.0 3.0 copy-start.1
  8.0 5.0 copy-start.49
  8.0 134.2 %all-gather.7.cloned.1.call-start = ((), (), s32[]{:S(2)}) async-start(), calls=%async_computation.10 | async-start | bytes 3932160 | tf_op jit(solution)/shard_map/all_gather | solution.py:161
  9.5 9.9 copy-start.62
  11.0 8.5 copy-start.55
  11.0 8.5 copy-start.51
  13.0 253.3 %reduce-scatter.13.cloned.1.call-start = ((), (), s32[]{:S(2)}) async-start(), calls=%async_computation.11 | async-start | bytes 7864320 | tf_op jit(solution)/shard_map/reduce_scatter | solution.py:167
  13.1 45.0 %collective-permute-start.1 = (bf16[192,96]{1,0:T(8,128)(2,1)S(1)}, bf16[192,96]{1,0:T(8,128)(2,1)S(1)}, u32[]{:S(2)}, u32[]{:S(2)}) collective-permute-start(bf16[192,96]{1,0:T(8,128)(2,1)S(1)} %copy-done.49), channel_id=1, source_target_pairs={{0,28},{4,0},{8,4},{12,8},{16,12},{20,16},{24,20},{28,24},{1,29},{... | collective-permute-start | bytes 110600 | tf_op jit(solution)/shard_map/ppermute | solution.py:200
  19.1 6.8 collective-permute-start
  22.4 3.5 copy-start.46
  22.4 39.5 %copy-start.47 = (bf16[96,192]{1,0:T(8,128)(2,1)S(1)}, bf16[96,192]{1,0:T(8,128)(2,1)}, u32[]{:S(2)}) copy-start(bf16[96,192]{1,0:T(8,128)(2,1)} %param.26) | copy-start | bytes 110596
  22.5 77.3 %copy-start.48 = (bf16[96,192]{1,0:T(8,128)(2,1)S(1)}, bf16[96,192]{1,0:T(8,128)(2,1)}, u32[]{:S(2)}) copy-start(bf16[96,192]{1,0:T(8,128)(2,1)} %param.27) | copy-start | bytes 110596
  25.9 36.1 %collective-permute-start.2 = (bf16[192,96]{1,0:T(8,128)(2,1)S(1)}, bf16[192,96]{1,0:T(8,128)(2,1)S(1)}, u32[]{:S(2)}, u32[]{:S(2)}) collective-permute-start(bf16[192,96]{1,0:T(8,128)(2,1)S(1)} %collective-permute-done), channel_id=1, source_target_pairs={{0,4},{4,8},{8,12},{12,16},{16,20},{20,24},{24,28},{28,0},{1,5},{5... | collective-permute-start | bytes 110600 | tf_op jit(solution)/shard_map/ppermute | solution.py:193
  58.1 103.6 %copy-start.20 = (bf16[768,192]{1,0:T(8,128)(2,1)}, bf16[768,192]{1,0:T(8,128)(2,1)S(1)}, u32[]{:S(2)}) copy-start(bf16[768,192]{1,0:T(8,128)(2,1)S(1)} %all_gather.29) | copy-start | bytes 884740
  58.1 36.9 %collective-permute-start.3 = (bf16[192,96]{1,0:T(8,128)(2,1)S(1)}, bf16[192,96]{1,0:T(8,128)(2,1)S(1)}, u32[]{:S(2)}, u32[]{:S(2)}) collective-permute-start(bf16[192,96]{1,0:T(8,128)(2,1)S(1)} %collective-permute-done.1), channel_id=1, source_target_pairs={{0,28},{4,0},{8,4},{12,8},{16,12},{20,16},{24,20},{28,24},{1,29},{... | collective-permute-start | bytes 110600 | tf_op jit(solution)/shard_map/ppermute | solution.py:200
  62.0 37.8 %collective-permute-start.4 = (bf16[192,96]{1,0:T(8,128)(2,1)S(1)}, bf16[192,96]{1,0:T(8,128)(2,1)S(1)}, u32[]{:S(2)}, u32[]{:S(2)}) collective-permute-start(bf16[192,96]{1,0:T(8,128)(2,1)S(1)} %collective-permute-done.2), channel_id=1, source_target_pairs={{0,4},{4,8},{8,12},{12,16},{16,20},{20,24},{24,28},{28,0},{1,5},{5... | collective-permute-start | bytes 110600 | tf_op jit(solution)/shard_map/ppermute | solution.py:193
  95.0 45.6 %collective-permute-start.5 = (bf16[192,96]{1,0:T(8,128)(2,1)S(1)}, bf16[192,96]{1,0:T(8,128)(2,1)S(1)}, u32[]{:S(2)}, u32[]{:S(2)}) collective-permute-start(bf16[192,96]{1,0:T(8,128)(2,1)S(1)} %collective-permute-done.3), channel_id=1, source_target_pairs={{0,28},{4,0},{8,4},{12,8},{16,12},{20,16},{24,20},{28,24},{1,29},{... | collective-permute-start | bytes 110600 | tf_op jit(solution)/shard_map/ppermute | solution.py:200
  99.8 41.4 %collective-permute-start.6 = (bf16[192,96]{1,0:T(8,128)(2,1)S(1)}, bf16[192,96]{1,0:T(8,128)(2,1)S(1)}, u32[]{:S(2)}, u32[]{:S(2)}) collective-permute-start(bf16[192,96]{1,0:T(8,128)(2,1)S(1)} %collective-permute-done.4), channel_id=1, source_target_pairs={{0,4},{4,8},{8,12},{12,16},{16,20},{20,24},{24,28},{28,0},{1,5},{5... | collective-permute-start | bytes 110600 | tf_op jit(solution)/shard_map/ppermute | solution.py:193
  142.2 9.6 copy-start.8
  199.4 3.1 copy-start.37
  206.3 60.0 %copy-start.2 = (bf16[512,768]{1,0:T(8,128)(2,1)S(1)}, bf16[512,768]{1,0:T(8,128)(2,1)}, u32[]{:S(2)}) copy-start(bf16[512,768]{1,0:T(8,128)(2,1)} %param.21) | copy-start | bytes 2359300
  206.3 67.2 %all-gather.11.cloned.1.call-start = ((), (), s32[]{:S(2)}) async-start(), calls=%async_computation.13 | async-start | bytes 1327104 | tf_op jit(solution)/shard_map/all_gather | solution.py:215
  206.9 61.4 %copy-start.50 = (f32[768]{0:T(1024)S(1)}, f32[768]{0:T(1024)}, u32[]{:S(2)}) copy-start(f32[768]{0:T(1024)} %param.33) | copy-start | bytes 9220
  206.9 61.4 %copy-start.60 = (f32[768]{0:T(1024)S(1)}, f32[768]{0:T(1024)}, u32[]{:S(2)}) copy-start(f32[768]{0:T(1024)} %param.34) | copy-start | bytes 9220
  206.9 91.1 %all-gather.9.cloned.1.call-start = ((), (), s32[]{:S(2)}) async-start(), calls=%async_computation.12 | async-start | bytes 3932160 | tf_op jit(solution)/shard_map/all_gather | solution.py:161
  267.9 3.1 copy-start.13
  269.5 72.3 %all-gather.13.cloned.1.call-start = ((), (), s32[]{:S(2)}) async-start(), calls=%async_computation.14 | async-start | bytes 1327104 | tf_op jit(solution)/shard_map/all_gather | solution.py:216
  270.1 100.9 %all-gather.15.cloned.1.call-start = ((), (), s32[]{:S(2)}) async-start(), calls=%async_computation.16 | async-start | bytes 3932160 | tf_op jit(solution)/shard_map/all_gather | solution.py:164
  272.7 173.7 %reduce-scatter.17.cloned.1.call-start = ((), (), s32[]{:S(2)}) async-start(), calls=%async_computation.17 | async-start | bytes 7864320 | tf_op jit(solution)/shard_map/reduce_scatter | solution.py:178
  370.9 12.6 %copy-start.65 = (bf16[768,768]{1,0:T(8,128)(2,1)S(1)}, bf16[768,768]{1,0:T(8,128)(2,1)}, u32[]{:S(2)}) copy-start(bf16[768,768]{1,0:T(8,128)(2,1)} %all-gather.11.cloned.1.call-done) | copy-start | bytes 3538948
  388.1 119.2 %reduce-scatter.15.cloned.1.call-start = ((), (), s32[]{:S(2)}) async-start(), calls=%async_computation.15 | async-start | bytes 7864320 | tf_op jit(solution)/shard_map/reduce_scatter | solution.py:167
  396.1 111.1 %copy-start.61 = (f32[768]{0:T(1024)S(1)}, f32[768]{0:T(1024)}, u32[]{:S(2)}) copy-start(f32[768]{0:T(1024)} %param.36) | copy-start | bytes 9220
  396.1 151.9 %all-gather.17.cloned.1.call-start = ((), (), s32[]{:S(2)}) async-start(), calls=%async_computation.18 | async-start | bytes 3932160 | tf_op jit(solution)/shard_map/all_gather | solution.py:164
  507.2 8.4 copy-start.16
  516.3 3.5 copy-start.53
  519.3 153.9 %reduce-scatter.31.cloned.1.call-start = ((), (), s32[]{:S(2)}) async-start(), calls=%async_computation.25 | async-start | bytes 884736
  551.1 3.8 copy-start.5
  551.1 3.8 copy-start.7
  551.1 3.8 copy-start.15
  561.8 7.2 copy-start.28
  569.0 7.1 copy-start.30
  587.4 7.2 copy-start.28
  594.6 7.1 copy-start.30
  606.1 4.8 copy-start.32
  606.1 4.8 copy-start.35
  606.1 4.8 copy-start.39
  606.2 4.8 copy-start.40
  610.7 122.9 %reduce-scatter.19.cloned.1.call-start = ((), (), s32[]{:S(2)}) async-start(), calls=%async_computation.19 | async-start | bytes 7864320 | tf_op jit(solution)/shard_map/reduce_scatter | solution.py:178
  622.0 185.2 %reduce-scatter.27.cloned.1.call-start = ((), (), s32[]{:S(2)}) async-start(), calls=%async_computation.23 | async-start | bytes 2654208 | tf_op jit(solution)/shard_map/reduce_scatter | solution.py:287
  629.9 249.9 %reduce-scatter.29.cloned.1.call-start = ((), (), s32[]{:S(2)}) async-start(), calls=%async_computation.24 | async-start | bytes 2654208 | tf_op jit(solution)/shard_map/reduce_scatter | solution.py:288
  630.2 7.2 copy-start.9
  637.3 308.3 %reduce-scatter.25.cloned.1.call-start = ((), (), s32[]{:S(2)}) async-start(), calls=%async_computation.22 | async-start | bytes 884736 | tf_op jit(solution)/shard_map/reduce_scatter | solution.py:285
  640.5 3.2 copy-start.63
  640.5 370.6 %reduce-scatter.23.cloned.1.call-start = ((), (), s32[]{:S(2)}) async-start(), calls=%async_computation.21 | async-start | bytes 884736 | tf_op jit(solution)/shard_map/reduce_scatter | solution.py:284
  643.6 433.1 %reduce-scatter.21.cloned.1.call-start = ((), (), s32[]{:S(2)}) async-start(), calls=%async_computation.20 | async-start | bytes 884736 | tf_op jit(solution)/shard_map/reduce_scatter | solution.py:283
  644.0 89.6 %copy-start.3 = (bf16[512,768]{1,0:T(8,128)(2,1)S(1)}, bf16[512,768]{1,0:T(8,128)(2,1)}, u32[]{:S(2)}) copy-start(bf16[512,768]{1,0:T(8,128)(2,1)} %param.21) | copy-start | bytes 2359300
  644.0 89.6 %copy-start.44 = (f32[512]{0:T(512)S(1)}, f32[512]{0:T(512)}, u32[]{:S(2)}) copy-start(f32[512]{0:T(512)} %copy-done.43) | copy-start | bytes 6148
  644.0 89.6 %copy-start.45 = (f32[768]{0:T(1024)S(1)}, f32[768]{0:T(1024)}, u32[]{:S(2)}) copy-start(f32[768]{0:T(1024)} %param.31) | copy-start | bytes 9220
  648.0 87.6 %copy-start.56 = (f32[512]{0:T(512)S(1)}, f32[512]{0:T(512)}, u32[]{:S(2)}) copy-start(f32[512]{0:T(512)} %copy-done.55) | copy-start | bytes 6148
  648.0 87.6 %copy-start.52 = (f32[512]{0:T(512)S(1)}, f32[512]{0:T(512)}, u32[]{:S(2)}) copy-start(f32[512]{0:T(512)} %copy-done.51) | copy-start | bytes 6148
  674.9 61.5 %copy-start.14 = (bf16[512,768]{1,0:T(8,128)(2,1)S(1)}, bf16[512,768]{1,0:T(8,128)(2,1)}, u32[]{:S(2)}) copy-start(bf16[512,768]{1,0:T(8,128)(2,1)} %param.23) | copy-start | bytes 2359300
  674.9 61.5 %copy-start.54 = (f32[512]{0:T(512)S(1)}, f32[512]{0:T(512)}, u32[]{:S(2)}) copy-start(f32[512]{0:T(512)} %copy-done.53) | copy-start | bytes 6148
  736.5 12.4 %copy-start.57 = (f32[768]{0:T(1024)S(1)}, f32[768]{0:T(1024)}, u32[]{:S(2)}) copy-start(f32[768]{0:T(1024)} %get-tuple-element.185) | copy-start | bytes 9220
  736.5 12.4 %copy-start.58 = (f32[768]{0:T(1024)S(1)}, f32[768]{0:T(1024)}, u32[]{:S(2)}) copy-start(f32[768]{0:T(1024)} %get-tuple-element.190) | copy-start | bytes 9220
  (35 other events, 56.0 us)
Sparse Core Ops, SparseCore 0:
  13.1 31.2 all-gather.6
  206.4 59.8 reduce-scatter.12
  519.5 28.5 all-gather.16
Sparse Core Ops, SparseCore 1:
  209.0 42.9 all-gather.10
  269.6 28.3 all-gather.8
  300.3 41.5 all-gather.12
  344.0 26.8 all-gather.14
  388.1 58.2 reduce-scatter.16
  449.0 58.2 reduce-scatter.14
  610.8 62.4 reduce-scatter.30
  676.3 57.3 reduce-scatter.18
  737.9 69.3 reduce-scatter.26
  811.7 68.0 reduce-scatter.28
  883.9 61.6 reduce-scatter.24
  949.5 61.6 reduce-scatter.22
  1015.2 61.5 reduce-scatter.20
